TPU v7x, 128 devices: a whole 4x4x4 slice. The times are simulated.
128 devices in a mesh: doc: 2 (over core), coarse: 4 (over z), fine: 16 (over y, x).
Axes of the slice: x: 4, y: 4, z: 4, core: 2. Of those that a mesh axis runs over, the one named last changes fastest.
Arguments:
- q_light: bfloat16 [2, 8192, 1024], P('doc', ('coarse', 'fine')), may hold values from -8 to 8
- k_light: bfloat16 [2, 8192, 1024], P('doc', ('coarse', 'fine')), may hold values from -8 to 8
- v_light: bfloat16 [2, 8192, 1024], P('doc', ('coarse', 'fine')), may hold values from -6 to 6
- q_heavy: bfloat16 [2, 8192, 1024], P('doc', ('coarse', 'fine')), may hold values from -8 to 8
- k_heavy: bfloat16 [2, 8192, 1024], P('doc', ('coarse', 'fine')), may hold values from -8 to 8
- v_heavy: bfloat16 [2, 8192, 1024], P('doc', ('coarse', 'fine')), may hold values from -6 to 6
- enc_kv: bfloat16 [2, 8192, 128], P('doc', ('coarse', 'fine')), may hold values from -8 to 8
- dec_queries: bfloat16 [2, 512, 1024], P('doc'), may hold values from -8 to 8
- query_ids: int32 [2, 64], P('doc'), may hold values from 0 to 63, as said below
- key_ids: int32 [2, 32], P('doc'), may hold values from 0 to 63, as said below
Outputs:
- encoded: bfloat16 [2, 8192, 1024], P('doc', ('coarse', 'fine'))
- decoded: bfloat16 [2, 512, 1024], P('doc')
Inputs may be any that keep to these rules, and one draw needn't show every extreme that they name: `query_ids`: for each document and each c below the number of coarse groups, entries c * 16 to (c + 1) * 16 - 1 are distinct block numbers among blocks c * 16 to (c + 1) * 16 - 1 (so every block of the group is listed), and entry c * 16 + f is the block assigned to the f-th device of that group. `key_ids`: for each document and each c below the number of coarse groups, entries c * 8 to (c + 1) * 8 - 1 are distinct block numbers among blocks c * 16 * 1 to (c + 1) * 16 - 1.
All inputs are finite; a program needn't handle non-finite values.
Results may differ from a plain program's by a relative error of at most 0.009.
Values may be sent and summed in bfloat16 or wider, within the bound.
No kernel may reach another device: no remote copies, remote signals or barrier semaphores. Data moves between devices by JAX's collectives and lax.ppermute only.
A program may use at most 384 MiB of HBM per device.

v0:
```python
import jax
import jax.numpy as jnp
from jax import lax
from jax.sharding import Mesh
from jax.sharding import PartitionSpec as P

HEAD = 64
ROUTED_BLOCK = 128
KGRP = 8
COARSE_FINE = ("coarse", "fine_0", "fine_1")
FINE = ("fine_0", "fine_1")


def extended(value, sides, width):
    edges = {}
    for axis, dim in sides:
        size, length = (lax.axis_size(axis), value.shape[dim])
        up = [(i, (i + 1) % size) for i in range(size - 1)]
        last = lax.slice_in_dim(value, length - width, length, axis=dim)
        first = lax.slice_in_dim(value, 0, width, axis=dim)
        edges[dim] = (
            lax.ppermute(last, axis, up),
            lax.ppermute(first, axis, [(b, a) for a, b in up]),
        )
    done = []
    for _, dim in sides:
        low, high = edges[dim]
        around = [(width, width) if d in done else (0, 0) for d in range(value.ndim)]
        value = jnp.concatenate([jnp.pad(low, around), value, jnp.pad(high, around)], axis=dim)
        done.append(dim)
    return value


def split_up(value, dim, length):
    lengths = value.shape
    pieces = value.reshape(*lengths[:dim], length, lengths[dim] // length, *lengths[dim + 1 :])
    return jnp.moveaxis(pieces, dim, 0)


def sum_at_owner(value, axis, dim):
    pieces = split_up(value, dim, lax.axis_size(axis))
    arrived = lax.all_to_all(pieces, axis, split_axis=0, concat_axis=0, tiled=True)
    return arrived.astype(jnp.float32).sum(axis=0)


def joined_all(value, axes, combine):
    for axis in axes:
        pieces = jax.tree.map(lambda part: lax.all_gather(part, axis), value)
        value = jax.tree.map(lambda part: part[0], pieces)
        for k in range(1, lax.axis_size(axis)):
            value = combine(value, jax.tree.map(lambda part: part[k], pieces))
    return value


def attend(query, keys, value_rows, mask):
    rows = query.shape[0]
    count = keys.shape[0]
    heads = query.shape[1] // HEAD
    qh = query.reshape(rows, heads, HEAD).transpose(1, 0, 2)
    kh = keys.reshape(count, heads, HEAD).transpose(1, 0, 2)
    vh = value_rows.reshape(count, heads, HEAD).transpose(1, 0, 2)

    def one_head(triple):
        qa, ka, va = triple
        scores = jnp.dot(qa, ka.T, preferred_element_type=jnp.float32) * HEAD ** (-0.5)
        if mask is not None:
            scores = jnp.where(mask, scores, jnp.float32(-1e30))
        peak = jnp.max(scores, axis=1, keepdims=True)
        weights = jnp.exp(scores - peak)
        weights = (weights / jnp.sum(weights, axis=1, keepdims=True)).astype(jnp.bfloat16)
        return jnp.dot(weights, va, preferred_element_type=jnp.float32)

    out = lax.map(one_head, (qh, kh, vh))
    return out.transpose(1, 0, 2).reshape(rows, heads * HEAD)


def combine(leading_entry, second):
    peak = jnp.maximum(leading_entry[0], second[0])
    scale_a = jnp.exp(leading_entry[0] - peak)
    scale_b = jnp.exp(second[0] - peak)
    total = leading_entry[1] * scale_a + second[1] * scale_b
    value_rows = leading_entry[2] * scale_a[..., None] + second[2] * scale_b[..., None]
    return (peak, total, value_rows)


def local(
    q_light, k_light, v_light, q_heavy, k_heavy, v_heavy, enc_kv, dec_queries, query_ids, key_ids
):
    query = q_light[0]
    tokens, width = query.shape
    n_seq = lax.axis_size(COARSE_FINE)
    n_fine = lax.axis_size(FINE)
    here = lax.axis_index(COARSE_FINE)
    group = lax.axis_index("coarse")
    start = here * tokens
    light_kv = jnp.concatenate([k_light[0], v_light[0]], axis=1)
    padded = extended(light_kv, ((COARSE_FINE, 0),), ROUTED_BLOCK)
    key_pos = start - ROUTED_BLOCK + jnp.arange(tokens + 2 * ROUTED_BLOCK, dtype=jnp.int32)
    inside = (key_pos >= 0) & (key_pos < tokens * n_seq)
    rows = min(512, tokens)
    qpos = start + 0 + jnp.arange(rows, dtype=jnp.int32)
    mask = (jnp.abs(qpos[:, None] - key_pos[None, :]) <= ROUTED_BLOCK - 1) & inside[None, :]
    pieces = attend(query, padded[:, :width], padded[:, width:], mask)
    blocks = tokens // ROUTED_BLOCK
    mine = here * blocks + jnp.arange(blocks, dtype=jnp.int32)
    key_group = lax.dynamic_slice_in_dim(key_ids[0], group * KGRP, KGRP)
    pick_keys = (key_group[:, None] == mine[None, :]).astype(jnp.bfloat16)
    heavy_kv = jnp.concatenate([k_heavy[0], v_heavy[0]], axis=1).reshape(
        blocks, ROUTED_BLOCK, 2 * width
    )
    slots = jnp.einsum(
        "sb,bre->sre", pick_keys, heavy_kv, preferred_element_type=jnp.float32
    ).reshape(KGRP * ROUTED_BLOCK, 2 * width)
    share = sum_at_owner(slots.astype(jnp.bfloat16), FINE, 0).astype(jnp.bfloat16)
    keys_all = lax.all_gather(share, COARSE_FINE, axis=0, tiled=True)
    query_group = lax.dynamic_slice_in_dim(query_ids[0], group * n_fine, n_fine)
    pick_rows = (query_group[:, None] == mine[None, :]).astype(jnp.bfloat16)
    heavy_query = q_heavy[0]
    result = attend(heavy_query, keys_all[:, :width], keys_all[:, width:], None).astype(
        jnp.bfloat16
    )
    chosen = jnp.sum(pick_rows.astype(jnp.float32), axis=0)
    heavy = (
        result.reshape(blocks, ROUTED_BLOCK, width).astype(jnp.float32) * chosen[:, None, None]
    ).reshape(tokens, width)
    encoded = (pieces + heavy).astype(jnp.bfloat16)[None]
    decoder_query_rows = dec_queries[0]
    count = decoder_query_rows.shape[0]
    heads = width // HEAD
    enc_keys = enc_kv[0][:, :HEAD]
    enc_values = enc_kv[0][:, HEAD:]
    heads_query = decoder_query_rows.reshape(count, heads, HEAD).transpose(1, 0, 2)

    def partial_head(qa):
        scores = jnp.dot(qa, enc_keys.T, preferred_element_type=jnp.float32) * HEAD ** (-0.5)
        peak = jnp.max(scores, axis=1)
        weights = jnp.exp(scores - peak[:, None])
        total = jnp.sum(weights, axis=1)
        value_rows = jnp.dot(
            weights.astype(jnp.bfloat16), enc_values, preferred_element_type=jnp.float32
        )
        return (peak, total, value_rows)

    peak, total, value_rows = lax.map(partial_head, heads_query)
    peak, total, value_rows = joined_all((peak, total, value_rows), COARSE_FINE, combine)
    decoded = (
        (value_rows / total[..., None])
        .transpose(1, 0, 2)
        .reshape(count, width)
        .astype(jnp.bfloat16)[None]
    )
    return (encoded, decoded)


def solution(mesh):
    torus = Mesh(
        mesh.devices.reshape(mesh.shape["doc"], mesh.shape["coarse"], 4, 4),
        ("doc", "coarse", "fine_0", "fine_1"),
    )
    return jax.shard_map(
        local,
        mesh=torus,
        in_specs=(
            P("doc", COARSE_FINE, None),
            P("doc", COARSE_FINE, None),
            P("doc", COARSE_FINE, None),
            P("doc", COARSE_FINE, None),
            P("doc", COARSE_FINE, None),
            P("doc", COARSE_FINE, None),
            P("doc", COARSE_FINE, None),
            P("doc", None, None),
            P("doc", None),
            P("doc", None),
        ),
        out_specs=(P("doc", COARSE_FINE, None), P("doc", None, None)),
        check_vma=False,
    )
```

profile of v0, /device:TPU:1, one launch (start us, length us, event | category | flops | bytes accessed | tf_op | source)
XLA Modules:
  0.0 475.2 jit_solution(11982831535126823827)
XLA Ops:
  8.8 19.9 %while.39 = (s32[]{:T(128)}, f32[16,512]{1,0:T(8,128)S(1)}, f32[16,512]{1,0:T(8,128)S(1)}, f32[16,512,64]{1,2,0:T(8,128)}, bf16[16,512,64]{1,2,0:T(8,128)(2,1)S(...) while((s32[]{:T(128)}, f32[16,512]{1,0:T(8,128)S(1)}, ...), condition=%wide.region_13.14_spmd.clone, body=%wide.region_10.13_spmd.sunk.clone | while | flops 17169408 | bytes 1048677 | solution.py:144
  28.9 11.6 %all-gather.1 = f32[64,512]{1,0:T(8,128)S(1)} all-gather(f32[16,512]{1,0:T(8,128)S(1)} %get-tuple-element.103), channel_id=3, replica_groups=mesh['doc'=2,'coarse'=4,'fine_0'=4,'fine_1'=4] {'coarse'}, dimensions={0}, use_global_device_ids=true | all-gather | bytes 163840 | tf_op jit(solution)/shard_map/all_gather | solution.py:48
  40.5 75.0 %all-gather.14.cloned.1.call-done = f32[64,512,64]{1,2,0:T(8,128)} async-done(((f32[16,512,64]{1,2,0:T(8,128)}), f32[64,512,64]{1,2,0:T(8,128)}) %all-gather.14.cloned.1.call-update) | async-done | bytes 8388624 | tf_op jit(solution)/shard_map/all_gather | solution.py:48
  115.5 6.3 %fusion.50 = f32[1,16,512,64]{2,3,1,0:T(8,128)} fusion(f32[64,512,64]{1,2,0:T(8,128)} %all-gather.14.cloned.1.call-done, f32[16,512]{1,0:T(8,128)S(1)} %get-tuple-element.266, f32[16,512]{1,0:T(8,128)S(1)} %get-tuple-element.263, f32[16,512]{1,0:T(8,128)S(1)} %get-tuple-element.265, f32[16,512]{1,0:T(8,128)S(1)} %get-tuple-element.264, ...), kind=kLoop, calls=%fused_computation.70 | loop fusion | flops 4718592 | bytes 10682368 | tf_op jit(solution)/shard_map/add | solution.py:82
  124.2 61.8 %all_to_all.5 = bf16[16,64,2048]{2,1,0:T(8,128)(2,1)} all-to-all(bf16[16,64,2048]{2,1,0:T(8,128)(2,1)S(1)} %bitcast.387), channel_id=1, replica_groups=mesh['doc'=2,'coarse'=4,'fine_0'=4,'fine_1'=4] {'fine_0','fine_1'}, dimensions={0} | all-to-all | bytes 8388608 | tf_op jit(solution)/shard_map/all_to_all | solution.py:42
  185.9 3.9 reduce_sum.48
  191.6 5.0 %collective-permute-start = (bf16[128,2048]{0,1:T(8,128)(2,1)S(1)}, bf16[128,2048]{0,1:T(8,128)(2,1)S(1)}, u32[]{:S(2)}, u32[]{:S(2)}) collective-permute-start(bf16[128,2048]{0,1:T(8,128)(2,1)S(1)} %pad_maximum_fusion.1), channel_id=1, source_target_pairs={{0,1},{1,2},{2,3},{3,4},{4,5},{5,6},{6,7},{7,8},{8,9},{9,10},{10,1... | collective-permute-start | bytes 1572872 | tf_op jit(solution)/shard_map/ppermute | solution.py:22
  196.6 19.3 %all-gather.2 = f32[64,512]{1,0:T(8,128)S(1)} all-gather(f32[16,512]{1,0:T(8,128)S(1)} %get-tuple-element.104), channel_id=4, replica_groups=mesh['doc'=2,'coarse'=4,'fine_0'=4,'fine_1'=4] {'coarse'}, dimensions={0}, use_global_device_ids=true | all-gather | bytes 163840 | tf_op jit(solution)/shard_map/all_gather | solution.py:48
  215.9 10.7 %all_gather.51 = f32[4,16,512]{2,1,0:T(8,128)S(1)} all-gather(f32[1,16,512]{2,1,0:T(8,128)S(1)} %get-tuple-element.242), channel_id=1, replica_groups=mesh['doc'=2,'coarse'=4,'fine_0'=4,'fine_1'=4] {'fine_0'}, dimensions={0}, use_global_device_ids=true | all-gather | bytes 163840 | tf_op jit(solution)/shard_map/all_gather | solution.py:48
  226.6 10.7 %all_gather.56 = f32[4,16,512]{2,1,0:T(8,128)S(1)} all-gather(f32[1,16,512]{2,1,0:T(8,128)S(1)} %get-tuple-element.241), channel_id=1, replica_groups=mesh['doc'=2,'coarse'=4,'fine_0'=4,'fine_1'=4] {'fine_0'}, dimensions={0}, use_global_device_ids=true | all-gather | bytes 163840 | tf_op jit(solution)/shard_map/all_gather | solution.py:48
  238.1 10.3 %all_gather.57 = f32[4,16,512]{2,1,0:T(8,128)S(1)} all-gather(f32[1,16,512]{2,1,0:T(8,128)S(1)} %get-tuple-element.239), channel_id=1, replica_groups=mesh['doc'=2,'coarse'=4,'fine_0'=4,'fine_1'=4] {'fine_1'}, dimensions={0}, use_global_device_ids=true | all-gather | bytes 163840 | tf_op jit(solution)/shard_map/all_gather | solution.py:48
  249.3 1.8 copy.50
  251.7 9.7 %all_gather.53 = f32[4,16,512]{2,1,0:T(8,128)S(1)} all-gather(f32[1,16,512]{2,1,0:T(8,128)S(1)} %get-tuple-element.240), channel_id=1, replica_groups=mesh['doc'=2,'coarse'=4,'fine_0'=4,'fine_1'=4] {'fine_1'}, dimensions={0}, use_global_device_ids=true | all-gather | bytes 163840 | tf_op jit(solution)/shard_map/all_gather | solution.py:48
  263.2 24.0 %while.40 = (s32[]{:T(128)}, f32[16,128,64]{1,2,0:T(8,128)S(1)}, bf16[16,128,64]{1,2,0:T(8,128)(2,1)}, bf16[16,384,64]{1,2,0:T(8,128)(2,1)S(1)}, bf16[16,384,64]...) while((s32[]{:T(128)}, f32[16,128,64]{1,2,0:T(8,128)S(1)}, ...), condition=%wide.region_3.4_spmd.clone.clone, body=%wide.region_0.3_spmd.clone.sunk.clone | while | flops 13172482 | bytes 745053 | solution.py:73
  287.3 6.3 %fusion.44 = f32[1,16,512,64]{2,3,1,0:T(8,128)} fusion(f32[4,16,512,64]{2,3,1,0:T(8,128)} %all-gather.10.cloned.1.call-done, f32[16,512]{1,0:T(8,128)S(1)} %copy-done.9, f32[16,512]{1,0:T(8,128)S(1)} %copy-done.6, f32[16,512]{1,0:T(8,128)S(1)} %copy-done.8, f32[16,512]{1,0:T(8,128)S(1)} %copy-done.7, f32[16,512]{1,0:T(8,128)S(1)} %copy-done.5, ...), kind=kLoop, calls=%fused_computation.60 | loop fusion | flops 4718592 | bytes 10682368 | tf_op jit(solution)/shard_map/add | solution.py:82
  293.6 73.1 %all-gather.8.cloned.1.call-done = bf16[4096,2048]{1,0:T(8,128)(2,1)} async-done(((bf16[64,2048]{1,0:T(8,128)(2,1)}), bf16[4096,2048]{1,0:T(8,128)(2,1)}) %all-gather.8.cloned.1.call-update) | async-done | bytes 16777232 | tf_op jit(solution)/shard_map/all_gather | solution.py:115
  366.7 12.0 %fusion.107 = (bf16[4096,1024]{1,0:T(8,128)(2,1)}, bf16[4096,1024]{1,0:T(8,128)(2,1)}) fusion(bf16[4096,2048]{1,0:T(8,128)(2,1)} %all-gather.8.cloned.1.call-done), kind=kLoop, calls=%fused_computation.185 | loop fusion | bytes 33554432 | tf_op jit(solution)/shard_map/slice | solution.py:119
  378.7 11.5 %copy.67 = bf16[4096,1024]{0,1:T(8,128)(2,1)} copy(bf16[4096,1024]{1,0:T(8,128)(2,1)} %get-tuple-element.254) | data formatting | bytes 16777216
  390.2 11.4 %copy.68 = bf16[4096,1024]{0,1:T(8,128)(2,1)} copy(bf16[4096,1024]{1,0:T(8,128)(2,1)} %get-tuple-element.253) | data formatting | bytes 16777216
  401.7 59.1 %while.38 = (s32[]{:T(128)}, bf16[16,128,64]{1,2,0:T(8,128)(2,1)S(1)}, bf16[16,128,64]{1,2,0:T(8,128)(2,1)}, bf16[16,4096,64]{1,2,0:T(8,128)(2,1)}, bf16[16,4096,64]{1,2,0:T(8,128)(2,1)}) while((s32[]{:T(128)}, bf16[16,128,64]{1,2,0:T(8,128)(2,1)S(1)}, bf16[16,128,64]{1,2,0:T(8,128)(2,1)}, bf16[16,4096,64]{1,2,0:T(8,128)(2,1)}, ...), condition=%wide.region_8.9_spmd.clone, body=%wide.region_5.8_spmd.sunk.clone | while | flops 137887488 | bytes 7393861 | solution.py:73
  401.7 1.7 fusion.141
  403.8 1.6 fusion.143
  407.5 1.6 fusion.143
  409.1 1.6 fusion.141
  411.2 1.6 fusion.143
  412.8 1.6 fusion.141
  414.9 1.6 fusion.143
  416.5 1.6 fusion.141
  418.6 1.6 fusion.143
  420.2 1.6 fusion.141
  422.3 1.6 fusion.143
  423.9 1.6 fusion.141
  426.0 1.6 fusion.143
  427.6 1.6 fusion.141
  429.6 1.6 fusion.143
  431.3 1.6 fusion.141
  433.3 1.6 fusion.143
  435.0 1.6 fusion.141
  437.0 1.6 fusion.143
  438.7 1.6 fusion.141
  440.7 1.6 fusion.143
  442.4 1.6 fusion.141
  444.4 1.6 fusion.143
  448.1 1.6 fusion.143
  451.8 1.6 fusion.143
  455.5 1.6 fusion.143
  459.2 1.6 fusion.143
  462.4 5.0 %fusion.58 = bf16[16,512,64]{1,2,0:T(8,128)(2,1)S(1)} fusion(f32[4,16,512,64]{2,3,1,0:T(8,128)} %all-gather.12.cloned.1.call-done, f32[16,512]{1,0:T(8,128)S(1)} %copy-done.11, f32[16,512]{1,0:T(8,128)S(1)} %copy-done.17, f32[16,512]{1,0:T(8,128)S(1)} %copy-done.16, f32[16,512]{1,0:T(8,128)S(1)} %copy-done.15, f32[16,512]{1,0:T(8,128)S(1)} %copy-done.14, ...), kind=kLoop, calls=%fused_computation.81 | loop fusion | flops 5767168 | bytes 9666560 | tf_op jit(solution)/shard_map/convert_element_type | solution.py:150
  (234 shorter events, 70.9 us)
Async XLA Ops:
  7.2 1.6 copy-start.18
  7.2 108.3 %all-gather.14.cloned.1.call-start = ((), (), s32[]{:S(2)}) async-start(), calls=%async_computation.4 | async-start | bytes 10485760 | tf_op jit(solution)/shard_map/all_gather | solution.py:48
  28.8 258.4 %all-gather.10.cloned.1.call-start = ((), (), s32[]{:S(2)}) async-start(), calls=%async_computation.2 | async-start | bytes 10485760 | tf_op jit(solution)/shard_map/all_gather | solution.py:48
  121.8 0.7 copy-start.19
  121.8 1.0 copy-start.3
  121.8 1.0 copy-start.4
  121.8 244.8 %all-gather.8.cloned.1.call-start = ((), (), s32[]{:S(2)}) async-start(), calls=%async_computation.1 | async-start | bytes 17039360 | tf_op jit(solution)/shard_map/all_gather | solution.py:115
  185.9 3.9 copy-start
  185.9 4.1 copy-start.1
  189.8 58.6 %copy-start.2 = (bf16[1,128,1024]{2,1,0:T(8,128)(2,1)S(1)}, bf16[1,128,1024]{2,1,0:T(8,128)(2,1)}, u32[]{:S(2)}) copy-start(bf16[1,128,1024]{2,1,0:T(8,128)(2,1)} %param.16) | copy-start | bytes 786436
  189.8 272.5 %all-gather.12.cloned.1.call-start = ((), (), s32[]{:S(2)}) async-start(), calls=%async_computation.3 | async-start | bytes 10485760 | tf_op jit(solution)/shard_map/all_gather | solution.py:48
  190.1 61.0 %copy-start.20 = (s32[1,64]{1,0:T(1,128)S(1)}, s32[1,64]{1,0:T(1,128)}, u32[]{:S(2)}) copy-start(s32[1,64]{1,0:T(1,128)} %param.24) | copy-start | bytes 772
  190.3 72.5 %collective-permute-start.1 = (bf16[128,2048]{0,1:T(8,128)(2,1)S(1)}, bf16[128,2048]{0,1:T(8,128)(2,1)S(1)}, u32[]{:S(2)}, u32[]{:S(2)}) collective-permute-start(bf16[128,2048]{0,1:T(8,128)(2,1)S(1)} %pad_maximum_fusion.1), channel_id=1, source_target_pairs={{1,0},{2,1},{3,2},{4,3},{5,4},{6,5},{7,6},{8,7},{9,8},{10,9},{11,1... | collective-permute-start | bytes 1572872 | tf_op jit(solution)/shard_map/ppermute | solution.py:23
  191.6 71.2 %collective-permute-start = (bf16[128,2048]{0,1:T(8,128)(2,1)S(1)}, bf16[128,2048]{0,1:T(8,128)(2,1)S(1)}, u32[]{:S(2)}, u32[]{:S(2)}) collective-permute-start(bf16[128,2048]{0,1:T(8,128)(2,1)S(1)} %pad_maximum_fusion.1), channel_id=1, source_target_pairs={{0,1},{1,2},{2,3},{3,4},{4,5},{5,6},{6,7},{7,8},{8,9},{9,10},{10,1... | collective-permute-start | bytes 1572872 | tf_op jit(solution)/shard_map/ppermute | solution.py:22
  263.2 24.1 %copy-start.5 = (f32[16,512]{1,0:T(8,128)S(1)}, f32[16,512]{1,0:T(8,128)}, u32[]{:S(2)}) copy-start(f32[16,512]{1,0:T(8,128)} %get-tuple-element.257) | copy-start | bytes 98308
  263.2 24.1 %copy-start.6 = (f32[16,512]{1,0:T(8,128)S(1)}, f32[16,512]{1,0:T(8,128)}, u32[]{:S(2)}) copy-start(f32[16,512]{1,0:T(8,128)} %get-tuple-element.258) | copy-start | bytes 98308
  263.2 24.1 %copy-start.7 = (f32[16,512]{1,0:T(8,128)S(1)}, f32[16,512]{1,0:T(8,128)}, u32[]{:S(2)}) copy-start(f32[16,512]{1,0:T(8,128)} %get-tuple-element.259) | copy-start | bytes 98308
  263.2 24.1 %copy-start.8 = (f32[16,512]{1,0:T(8,128)S(1)}, f32[16,512]{1,0:T(8,128)}, u32[]{:S(2)}) copy-start(f32[16,512]{1,0:T(8,128)} %get-tuple-element.260) | copy-start | bytes 98308
  263.2 24.1 %copy-start.9 = (f32[16,512]{1,0:T(8,128)S(1)}, f32[16,512]{1,0:T(8,128)}, u32[]{:S(2)}) copy-start(f32[16,512]{1,0:T(8,128)} %get-tuple-element.261) | copy-start | bytes 98308
  263.2 24.1 %copy-start.10 = (f32[16,512]{1,0:T(8,128)S(1)}, f32[16,512]{1,0:T(8,128)}, u32[]{:S(2)}) copy-start(f32[16,512]{1,0:T(8,128)} %get-tuple-element.243) | copy-start | bytes 98308
  401.6 60.7 %copy-start.11 = (f32[16,512]{1,0:T(8,128)S(1)}, f32[16,512]{1,0:T(8,128)}, u32[]{:S(2)}) copy-start(f32[16,512]{1,0:T(8,128)} %get-tuple-element.232) | copy-start | bytes 98308
  401.6 60.7 %copy-start.12 = (f32[16,512]{1,0:T(8,128)S(1)}, f32[16,512]{1,0:T(8,128)}, u32[]{:S(2)}) copy-start(f32[16,512]{1,0:T(8,128)} %get-tuple-element.233) | copy-start | bytes 98308
  401.6 60.7 %copy-start.13 = (f32[16,512]{1,0:T(8,128)S(1)}, f32[16,512]{1,0:T(8,128)}, u32[]{:S(2)}) copy-start(f32[16,512]{1,0:T(8,128)} %get-tuple-element.234) | copy-start | bytes 98308
  401.6 60.7 %copy-start.14 = (f32[16,512]{1,0:T(8,128)S(1)}, f32[16,512]{1,0:T(8,128)}, u32[]{:S(2)}) copy-start(f32[16,512]{1,0:T(8,128)} %get-tuple-element.235) | copy-start | bytes 98308
  401.6 60.7 %copy-start.15 = (f32[16,512]{1,0:T(8,128)S(1)}, f32[16,512]{1,0:T(8,128)}, u32[]{:S(2)}) copy-start(f32[16,512]{1,0:T(8,128)} %get-tuple-element.236) | copy-start | bytes 98308
  401.6 60.7 %copy-start.16 = (f32[16,512]{1,0:T(8,128)S(1)}, f32[16,512]{1,0:T(8,128)}, u32[]{:S(2)}) copy-start(f32[16,512]{1,0:T(8,128)} %get-tuple-element.237) | copy-start | bytes 98308
  401.6 60.7 %copy-start.17 = (f32[16,512]{1,0:T(8,128)S(1)}, f32[16,512]{1,0:T(8,128)}, u32[]{:S(2)}) copy-start(f32[16,512]{1,0:T(8,128)} %get-tuple-element.238) | copy-start | bytes 98308
Sparse Core Ops, SparseCore 0:
  28.9 86.5 all-gather.13
  122.0 138.5 all-gather.9
  263.4 103.2 all-gather.7
  368.2 82.6 all-gather.11
where the time goes:
time: 478 us; the launch traced here: 475 us
  waiting for transfers between devices  148 us (31%)
  blocking collectives  134 us (28%)
  matrix products  88.7 us (19%)
  local copies, waits for them, and re-layouts  44.7 us (9%)
  other arithmetic  37.9 us (8%)
  between operations  14.2 us (3%)
  starting transfers between devices  6.46 us (1%)
    all_gather x3, waiting for transfers between devices, joined_all(): pieces = jax.tree.map(lambda part: lax.all_gather(part, axis), value)  75 us
    all_gather x1, waiting for transfers between devices, local(): keys_all = lax.all_gather(share, COARSE_FINE, axis=0, tiled=True)  73.1 us
    all_gather x6, blocking collectives, joined_all(): pieces = jax.tree.map(lambda part: lax.all_gather(part, axis), value)  72.3 us
    all_to_all x1, blocking collectives, sum_at_owner(): lax.all_to_all(pieces, axis, split_axis=0, concat_axis=0, tiled=True)  61.8 us
    dot_general x32, matrix products, one_head(): jnp.dot(qa, ka.T, preferred_element_type=jnp.float32) * HEAD ** (-0.5)  42.1 us
    unnamed x51, local copies, waits for them, and re-layouts  30.5 us
    dot_general x32, matrix products, one_head(): return jnp.dot(weights, va, preferred_element_type=jnp.float32)  30 us
    dot_general x16, matrix products, partial_head(): jnp.dot(weights.astype(jnp.bfloat16), enc_values, preferred_element_type=...  13.8 us
  transfers between devices with their start and end apart: 6, of which 2 were waited for; matrix products, arithmetic and copies ran while one was open for 29% of the time, Pallas kernels for 0%

commit v1 on v0

--- a/solution.py
+++ b/solution.py
@@ -112,7 +112,9 @@
         "sb,bre->sre", pick_keys, heavy_kv, preferred_element_type=jnp.float32
     ).reshape(KGRP * ROUTED_BLOCK, 2 * width)
     share = sum_at_owner(slots.astype(jnp.bfloat16), FINE, 0).astype(jnp.bfloat16)
-    keys_all = lax.all_gather(share, COARSE_FINE, axis=0, tiled=True)
+    keys_all = jnp.concatenate(
+        lax.all_to_all(jnp.stack(lax.axis_size(COARSE_FINE) * [share]), COARSE_FINE, 0, 0), axis=0
+    )
     query_group = lax.dynamic_slice_in_dim(query_ids[0], group * n_fine, n_fine)
     pick_rows = (query_group[:, None] == mine[None, :]).astype(jnp.bfloat16)
     heavy_query = q_heavy[0]

time: 478 us -> 564 us (1.18)
  the two profiles are of different devices: /device:TPU:1 before, /device:TPU:66 now
where the time goes in v1:
time: 564 us; the launch traced here: 561 us
  blocking collectives  354 us (63%)
  matrix products  88.7 us (16%)
  local copies, waits for them, and re-layouts  52.2 us (9%)
  other arithmetic  37.1 us (7%)
  between operations  14.2 us (3%)
  starting transfers between devices  13.9 us (2%)
    all_gather x6, blocking collectives, joined_all(): pieces = jax.tree.map(lambda part: lax.all_gather(part, axis), value)  297 us
    all_to_all x1, blocking collectives, sum_at_owner(): lax.all_to_all(pieces, axis, split_axis=0, concat_axis=0, tiled=True)  56.9 us
    dot_general x32, matrix products, one_head(): jnp.dot(qa, ka.T, preferred_element_type=jnp.float32) * HEAD ** (-0.5)  42 us
    dot_general x32, matrix products, one_head(): return jnp.dot(weights, va, preferred_element_type=jnp.float32)  30 us
    slice x2, local copies, waits for them, and re-layouts, local(): keys_all[:, width:]  24.1 us
    dot_general x16, matrix products, partial_head(): jnp.dot(weights.astype(jnp.bfloat16), enc_values, preferred_element_type=...  13.9 us
    add x2, other arithmetic, combine(): leading_entry[2] * scale_a[..., None] + second[2] * scale_b[..., None]  12.6 us
    slice x1, local copies, waits for them, and re-layouts, local(): keys_all[:, :width]  11.3 us
  transfers between devices with their start and end apart: 6, of which 0 were waited for; matrix products, arithmetic and copies ran while one was open for 26% of the time, Pallas kernels for 0%

profile of v1, /device:TPU:66, one launch (start us, length us, event | category | flops | bytes accessed | tf_op | source)
XLA Modules:
  0.0 561.2 jit_solution(1260505417491260971)
XLA Ops:
  8.8 20.0 %while.39 = (s32[]{:T(128)}, f32[16,512]{1,0:T(8,128)S(1)}, f32[16,512]{1,0:T(8,128)S(1)}, f32[16,512,64]{1,2,0:T(8,128)}, bf16[16,512,64]{1,2,0:T(8,128)(2,1)S(...) while((s32[]{:T(128)}, f32[16,512]{1,0:T(8,128)S(1)}, ...), condition=%wide.region_13.14_spmd.clone, body=%wide.region_10.13_spmd.sunk.clone | while | flops 17169408 | bytes 1048677 | solution.py:146
  31.2 56.9 %all_to_all.10 = bf16[16,64,2048]{2,1,0:T(8,128)(2,1)} all-to-all(bf16[16,64,2048]{2,1,0:T(8,128)(2,1)S(1)} %bitcast.388), channel_id=1, replica_groups=mesh['doc'=2,'coarse'=4,'fine_0'=4,'fine_1'=4] {'fine_0','fine_1'}, dimensions={0} | all-to-all | bytes 8388608 | tf_op jit(solution)/shard_map/all_to_all | solution.py:42
  88.1 3.0 reduce_sum.48
  91.1 6.0 %stack.2 = bf16[64,64,2048]{2,1,0:T(8,128)(2,1)} broadcast(bf16[64,2048]{1,0:T(8,128)(2,1)S(1)} %reduce_sum.48), dimensions={1,2} | broadcast | bytes 17039360 | tf_op jit(solution)/shard_map/stack | solution.py:116
  97.1 8.0 %all-to-all-start.1 = ((bf16[64,64,2048]{2,1,0:T(8,128)(2,1)}), bf16[64,64,2048]{2,1,0:T(8,128)(2,1)}, u32[]{:S(2)}, u32[]{:S(2)}) async-start(bf16[64,64,2048]{2,1,0:T(8,128)(2,1)} %stack.2), calls=%async_computation.1 | async-start | bytes 33554432 | tf_op jit(solution)/shard_map/all_to_all | solution.py:116
  105.2 144.3 %all-gather.1 = f32[64,512]{1,0:T(8,128)S(1)} all-gather(f32[16,512]{1,0:T(8,128)S(1)} %get-tuple-element.103), channel_id=3, replica_groups=mesh['doc'=2,'coarse'=4,'fine_0'=4,'fine_1'=4] {'coarse'}, dimensions={0}, use_global_device_ids=true | all-gather | bytes 163840 | tf_op jit(solution)/shard_map/all_gather | solution.py:48
  249.6 6.3 %fusion.50 = f32[1,16,512,64]{2,3,1,0:T(8,128)} fusion(f32[64,512,64]{1,2,0:T(8,128)} %all-gather.11.cloned.1.call-done, f32[16,512]{1,0:T(8,128)S(1)} %get-tuple-element.288, f32[16,512]{1,0:T(8,128)S(1)} %get-tuple-element.285, f32[16,512]{1,0:T(8,128)S(1)} %get-tuple-element.287, f32[16,512]{1,0:T(8,128)S(1)} %get-tuple-element.286, ...), kind=kLoop, calls=%fused_computation.70 | loop fusion | flops 4718592 | bytes 10682368 | tf_op jit(solution)/shard_map/add | solution.py:82
  257.2 1.9 collective-permute-start.1
  259.2 3.9 collective-permute-start
  263.1 30.1 %all-gather.2 = f32[64,512]{1,0:T(8,128)S(1)} all-gather(f32[16,512]{1,0:T(8,128)S(1)} %get-tuple-element.104), channel_id=4, replica_groups=mesh['doc'=2,'coarse'=4,'fine_0'=4,'fine_1'=4] {'coarse'}, dimensions={0}, use_global_device_ids=true | all-gather | bytes 163840 | tf_op jit(solution)/shard_map/all_gather | solution.py:48
  293.2 49.8 %all_gather.47 = f32[4,16,512]{2,1,0:T(8,128)S(1)} all-gather(f32[1,16,512]{2,1,0:T(8,128)S(1)} %get-tuple-element.264), channel_id=1, replica_groups=mesh['doc'=2,'coarse'=4,'fine_0'=4,'fine_1'=4] {'fine_0'}, dimensions={0}, use_global_device_ids=true | all-gather | bytes 163840 | tf_op jit(solution)/shard_map/all_gather | solution.py:48
  343.0 12.8 %all_gather.52 = f32[4,16,512]{2,1,0:T(8,128)S(1)} all-gather(f32[1,16,512]{2,1,0:T(8,128)S(1)} %get-tuple-element.263), channel_id=1, replica_groups=mesh['doc'=2,'coarse'=4,'fine_0'=4,'fine_1'=4] {'fine_0'}, dimensions={0}, use_global_device_ids=true | all-gather | bytes 163840 | tf_op jit(solution)/shard_map/all_gather | solution.py:48
  356.6 47.8 %all_gather.53 = f32[4,16,512]{2,1,0:T(8,128)S(1)} all-gather(f32[1,16,512]{2,1,0:T(8,128)S(1)} %get-tuple-element.261), channel_id=1, replica_groups=mesh['doc'=2,'coarse'=4,'fine_0'=4,'fine_1'=4] {'fine_1'}, dimensions={0}, use_global_device_ids=true | all-gather | bytes 163840 | tf_op jit(solution)/shard_map/all_gather | solution.py:48
  405.2 1.8 copy.66
  407.7 12.2 %all_gather.49 = f32[4,16,512]{2,1,0:T(8,128)S(1)} all-gather(f32[1,16,512]{2,1,0:T(8,128)S(1)} %get-tuple-element.262), channel_id=1, replica_groups=mesh['doc'=2,'coarse'=4,'fine_0'=4,'fine_1'=4] {'fine_1'}, dimensions={0}, use_global_device_ids=true | all-gather | bytes 163840 | tf_op jit(solution)/shard_map/all_gather | solution.py:48
  421.7 23.9 %while.40 = (s32[]{:T(128)}, f32[16,128,64]{1,2,0:T(8,128)S(1)}, bf16[16,128,64]{1,2,0:T(8,128)(2,1)}, bf16[16,384,64]{1,2,0:T(8,128)(2,1)S(1)}, bf16[16,384,64]...) while((s32[]{:T(128)}, f32[16,128,64]{1,2,0:T(8,128)S(1)}, ...), condition=%wide.region_3.4_spmd.clone.clone, body=%wide.region_0.3_spmd.clone.sunk.clone | while | flops 13172482 | bytes 745053 | solution.py:73
  445.8 6.3 %fusion.44 = f32[1,16,512,64]{2,3,1,0:T(8,128)} fusion(f32[4,16,512,64]{2,3,1,0:T(8,128)} %all-gather.7.cloned.1.call-done, f32[16,512]{1,0:T(8,128)S(1)} %copy-done.9, f32[16,512]{1,0:T(8,128)S(1)} %copy-done.6, f32[16,512]{1,0:T(8,128)S(1)} %copy-done.8, f32[16,512]{1,0:T(8,128)S(1)} %copy-done.7, f32[16,512]{1,0:T(8,128)S(1)} %copy-done.5, ...), kind=kLoop, calls=%fused_computation.60 | loop fusion | flops 4718592 | bytes 10682368 | tf_op jit(solution)/shard_map/add | solution.py:82
  452.1 12.2 %fusion.107 = (bf16[4096,1024]{1,0:T(8,128)(2,1)}, bf16[4096,1024]{1,0:T(8,128)(2,1)}) fusion(bf16[4096,2048]{1,0:T(8,128)(2,1)} %bitcast.22), kind=kLoop, calls=%fused_computation.185 | loop fusion | bytes 33554432 | tf_op jit(solution)/shard_map/slice | solution.py:121
  464.3 11.3 %copy.67 = bf16[4096,1024]{0,1:T(8,128)(2,1)} copy(bf16[4096,1024]{1,0:T(8,128)(2,1)} %get-tuple-element.276) | data formatting | bytes 16777216 | tf_op jit(solution)/shard_map/slice | solution.py:121
  475.6 11.9 %copy.68 = bf16[4096,1024]{0,1:T(8,128)(2,1)} copy(bf16[4096,1024]{1,0:T(8,128)(2,1)} %get-tuple-element.275) | data formatting | bytes 16777216 | tf_op jit(solution)/shard_map/slice | solution.py:121
  487.6 59.1 %while.38 = (s32[]{:T(128)}, bf16[16,128,64]{1,2,0:T(8,128)(2,1)S(1)}, bf16[16,128,64]{1,2,0:T(8,128)(2,1)}, bf16[16,4096,64]{1,2,0:T(8,128)(2,1)}, bf16[16,4096,64]{1,2,0:T(8,128)(2,1)}) while((s32[]{:T(128)}, bf16[16,128,64]{1,2,0:T(8,128)(2,1)S(1)}, bf16[16,128,64]{1,2,0:T(8,128)(2,1)}, bf16[16,4096,64]{1,2,0:T(8,128)(2,1)}, ...), condition=%wide.region_8.9_spmd.clone, body=%wide.region_5.8_spmd.sunk.clone | while | flops 137887488 | bytes 7393861 | solution.py:73
  487.6 1.6 fusion.141
  489.7 1.6 fusion.143
  491.4 1.6 fusion.141
  493.4 1.6 fusion.143
  495.1 1.6 fusion.141
  497.1 1.6 fusion.143
  498.8 1.6 fusion.141
  500.8 1.6 fusion.143
  502.5 1.6 fusion.141
  504.5 1.6 fusion.143
  506.2 1.6 fusion.141
  508.2 1.6 fusion.143
  509.9 1.6 fusion.141
  511.9 1.6 fusion.143
  513.6 1.6 fusion.141
  515.6 1.6 fusion.143
  517.3 1.6 fusion.141
  519.3 1.6 fusion.143
  521.0 1.6 fusion.141
  523.0 1.6 fusion.143
  526.7 1.6 fusion.143
  530.4 1.6 fusion.143
  534.1 1.6 fusion.143
  537.7 1.6 fusion.143
  541.4 1.6 fusion.143
  545.1 1.6 fusion.143
  548.4 5.0 fusion.58
  (234 shorter events, 72.3 us)
Async XLA Ops:
  7.2 1.6 copy-start.18
  7.2 242.4 %all-gather.11.cloned.1.call-start = ((), (), s32[]{:S(2)}) async-start(), calls=%async_computation.4 | async-start | bytes 10485760 | tf_op jit(solution)/shard_map/all_gather | solution.py:48
  28.8 0.7 copy-start.19
  28.8 1.0 copy-start.3
  28.8 1.0 copy-start.4
  97.1 355.0 %all-to-all-start.1 = ((bf16[64,64,2048]{2,1,0:T(8,128)(2,1)}), bf16[64,64,2048]{2,1,0:T(8,128)(2,1)}, u32[]{:S(2)}, u32[]{:S(2)}) async-start(bf16[64,64,2048]{2,1,0:T(8,128)(2,1)} %stack.2), calls=%async_computation.1 | async-start | bytes 33554432 | tf_op jit(solution)/shard_map/all_to_all | solution.py:116
  105.1 340.6 %all-gather.7.cloned.1.call-start = ((), (), s32[]{:S(2)}) async-start(), calls=%async_computation.2 | async-start | bytes 10485760 | tf_op jit(solution)/shard_map/all_gather | solution.py:48
  255.9 0.9 copy-start
  255.9 1.1 copy-start.1
  255.9 148.5 %copy-start.2 = (bf16[1,128,1024]{2,1,0:T(8,128)(2,1)S(1)}, bf16[1,128,1024]{2,1,0:T(8,128)(2,1)}, u32[]{:S(2)}) copy-start(bf16[1,128,1024]{2,1,0:T(8,128)(2,1)} %param.16) | copy-start | bytes 786436
  255.9 292.4 %all-gather.9.cloned.1.call-start = ((), (), s32[]{:S(2)}) async-start(), calls=%async_computation.3 | async-start | bytes 10485760 | tf_op jit(solution)/shard_map/all_gather | solution.py:48
  257.0 150.0 %copy-start.20 = (s32[1,64]{1,0:T(1,128)S(1)}, s32[1,64]{1,0:T(1,128)}, u32[]{:S(2)}) copy-start(s32[1,64]{1,0:T(1,128)} %param.24) | copy-start | bytes 772
  257.2 164.1 %collective-permute-start.1 = (bf16[128,2048]{0,1:T(8,128)(2,1)S(1)}, bf16[128,2048]{0,1:T(8,128)(2,1)S(1)}, u32[]{:S(2)}, u32[]{:S(2)}) collective-permute-start(bf16[128,2048]{0,1:T(8,128)(2,1)S(1)} %pad_maximum_fusion.1), channel_id=1, source_target_pairs={{1,0},{2,1},{3,2},{4,3},{5,4},{6,5},{7,6},{8,7},{9,8},{10,9},{11,1... | collective-permute-start | bytes 1572872 | tf_op jit(solution)/shard_map/ppermute | solution.py:23
  259.2 162.1 %collective-permute-start = (bf16[128,2048]{0,1:T(8,128)(2,1)S(1)}, bf16[128,2048]{0,1:T(8,128)(2,1)S(1)}, u32[]{:S(2)}, u32[]{:S(2)}) collective-permute-start(bf16[128,2048]{0,1:T(8,128)(2,1)S(1)} %pad_maximum_fusion.1), channel_id=1, source_target_pairs={{0,1},{1,2},{2,3},{3,4},{4,5},{5,6},{6,7},{7,8},{8,9},{9,10},{10,1... | collective-permute-start | bytes 1572872 | tf_op jit(solution)/shard_map/ppermute | solution.py:22
  421.7 24.0 %copy-start.5 = (f32[16,512]{1,0:T(8,128)S(1)}, f32[16,512]{1,0:T(8,128)}, u32[]{:S(2)}) copy-start(f32[16,512]{1,0:T(8,128)} %get-tuple-element.279) | copy-start | bytes 98308
  421.7 24.0 %copy-start.6 = (f32[16,512]{1,0:T(8,128)S(1)}, f32[16,512]{1,0:T(8,128)}, u32[]{:S(2)}) copy-start(f32[16,512]{1,0:T(8,128)} %get-tuple-element.280) | copy-start | bytes 98308
  421.7 24.0 %copy-start.7 = (f32[16,512]{1,0:T(8,128)S(1)}, f32[16,512]{1,0:T(8,128)}, u32[]{:S(2)}) copy-start(f32[16,512]{1,0:T(8,128)} %get-tuple-element.281) | copy-start | bytes 98308
  421.7 24.0 %copy-start.8 = (f32[16,512]{1,0:T(8,128)S(1)}, f32[16,512]{1,0:T(8,128)}, u32[]{:S(2)}) copy-start(f32[16,512]{1,0:T(8,128)} %get-tuple-element.282) | copy-start | bytes 98308
  421.7 24.0 %copy-start.9 = (f32[16,512]{1,0:T(8,128)S(1)}, f32[16,512]{1,0:T(8,128)}, u32[]{:S(2)}) copy-start(f32[16,512]{1,0:T(8,128)} %get-tuple-element.283) | copy-start | bytes 98308
  421.7 24.0 %copy-start.10 = (f32[16,512]{1,0:T(8,128)S(1)}, f32[16,512]{1,0:T(8,128)}, u32[]{:S(2)}) copy-start(f32[16,512]{1,0:T(8,128)} %get-tuple-element.265) | copy-start | bytes 98308
  487.6 60.8 %copy-start.11 = (f32[16,512]{1,0:T(8,128)S(1)}, f32[16,512]{1,0:T(8,128)}, u32[]{:S(2)}) copy-start(f32[16,512]{1,0:T(8,128)} %get-tuple-element.254) | copy-start | bytes 98308
  487.6 60.8 %copy-start.12 = (f32[16,512]{1,0:T(8,128)S(1)}, f32[16,512]{1,0:T(8,128)}, u32[]{:S(2)}) copy-start(f32[16,512]{1,0:T(8,128)} %get-tuple-element.255) | copy-start | bytes 98308
  487.6 60.8 %copy-start.13 = (f32[16,512]{1,0:T(8,128)S(1)}, f32[16,512]{1,0:T(8,128)}, u32[]{:S(2)}) copy-start(f32[16,512]{1,0:T(8,128)} %get-tuple-element.256) | copy-start | bytes 98308
  487.6 60.8 %copy-start.14 = (f32[16,512]{1,0:T(8,128)S(1)}, f32[16,512]{1,0:T(8,128)}, u32[]{:S(2)}) copy-start(f32[16,512]{1,0:T(8,128)} %get-tuple-element.257) | copy-start | bytes 98308
  487.6 60.8 %copy-start.15 = (f32[16,512]{1,0:T(8,128)S(1)}, f32[16,512]{1,0:T(8,128)}, u32[]{:S(2)}) copy-start(f32[16,512]{1,0:T(8,128)} %get-tuple-element.258) | copy-start | bytes 98308
  487.6 60.8 %copy-start.16 = (f32[16,512]{1,0:T(8,128)S(1)}, f32[16,512]{1,0:T(8,128)}, u32[]{:S(2)}) copy-start(f32[16,512]{1,0:T(8,128)} %get-tuple-element.259) | copy-start | bytes 98308
  487.6 60.8 %copy-start.17 = (f32[16,512]{1,0:T(8,128)S(1)}, f32[16,512]{1,0:T(8,128)}, u32[]{:S(2)}) copy-start(f32[16,512]{1,0:T(8,128)} %get-tuple-element.260) | copy-start | bytes 98308
Sparse Core Ops, SparseCore 0:
  29.0 172.9 all-gather.10
  256.0 151.7 all-gather.6
  452.2 82.5 all-gather.8
